TPU v7x, 512 devices: a whole 4x8x8 slice. The times are simulated.
512 devices in a mesh: dp: 16 (over z_hi, x), expert: 32 (over z_lo, y, core).
Axes of the slice: x: 4, y: 8, z: 8 (z_hi: 4, z_lo: 2; z = z_hi * 2 + z_lo), core: 2. Of those that a mesh axis runs over, the one named last changes fastest.
Arguments:
- tokens: bfloat16 [6144, 6144], P('expert', 'dp'), may hold values from -6 to 6
- expert_of: int32 [6144], P('expert'), may hold values from 0 to 31, as said below
- router_weight: float32 [6144], P('expert'), may hold values from 0.2 to 1
- cotangent: bfloat16 [6144, 6144], P('expert', 'dp'), may hold values from -6 to 6
- gate_up_weight: bfloat16 [32, 2, 6144, 1024], P('expert', None, 'dp'), may hold values from -0.078125 to 0.078125
- down_weight: bfloat16 [32, 1024, 6144], P('expert', None, 'dp'), may hold values from -0.1875 to 0.1875
Outputs:
- layer_out: bfloat16 [6144, 6144], P('expert', 'dp')
- grad_tokens: bfloat16 [6144, 6144], P('expert', 'dp')
- grad_gate_up: bfloat16 [32, 2, 6144, 1024], P('expert', None, 'dp')
- grad_down: bfloat16 [32, 1024, 6144], P('expert', None, 'dp')
Inputs may be any that keep to these rules, and one draw needn't show every extreme that they name: `expert_of`: take the tokens in aligned blocks of 192, one block for each index of expert. One expert, the same for all blocks, is named by exactly 12 tokens of every block; every other expert is named by at most 9 tokens of a block, and in every block some other expert by exactly 9.
All inputs are finite; a program needn't handle non-finite values.
Results may differ from a plain program's by a relative error of at most 0.0058.
Values may be sent and summed in bfloat16 or wider, within the bound.
No kernel may reach another device: no remote copies, remote signals or barrier semaphores. Data moves between devices by JAX's collectives and lax.ppermute only.
A program may use at most 64 MiB of HBM per device.

v0:
```python
import jax
import jax.numpy as jnp
from jax import lax
from jax.sharding import Mesh, PartitionSpec as P

NX = 4
NZ = 4
TOKEN_AXES = ("zl", "y", "core")


def slots_of(expert_of, width, room):
    count = expert_of.shape[0]
    index = jnp.arange(count, dtype=jnp.int32)
    earlier = (expert_of[:, None] == expert_of[None, :]) & (index[None, :] < index[:, None])
    position = jnp.sum(earlier.astype(jnp.int32), axis=1)
    slot = expert_of * room + position
    return (slot[None, :] == jnp.arange(width, dtype=jnp.int32)[:, None]).astype(jnp.bfloat16)


def dot(a, b, dims):
    return lax.dot_general(a, b, (dims, ((), ())), preferred_element_type=jnp.float32)


def sum_blocks(blocks):
    b = [blocks[i].astype(jnp.float32) for i in range(blocks.shape[0])]
    return b[0] + b[1] + (b[2] + b[3])


def scatter_sum(partial):
    rows, width = partial.shape
    first = lax.all_to_all(partial.reshape(NX, rows // NX, width), "x", 0, 0, tiled=True)
    first = sum_blocks(first).astype(jnp.bfloat16)
    second = lax.all_to_all(first.reshape(NZ, rows // NX // NZ, width), "zh", 0, 0, tiled=True)
    return sum_blocks(second)


def gather_rows(part):
    return lax.all_gather(lax.all_gather(part, "zh", axis=0, tiled=True), "x", axis=0, tiled=True)


def shards(tokens, expert_of, router_weight, cotangent, gate_up_weight, down_weight):
    tok, feat = tokens.shape
    experts = 32
    room = 2 * tok // experts
    rows = experts * room
    w_gate = gate_up_weight[0, 0]
    w_up = gate_up_weight[0, 1]
    w_down = down_weight[0]
    ff = w_gate.shape[1]
    scaled = (router_weight[:, None] * cotangent.astype(jnp.float32)).astype(jnp.bfloat16)
    dispatch = slots_of(expert_of, rows, room)
    send = jnp.concatenate(
        [dot(dispatch, tokens, ((1,), (0,))), dot(dispatch, scaled, ((1,), (0,)))], axis=1
    ).astype(jnp.bfloat16)
    recv = lax.all_to_all(
        send.reshape(experts, room, 2 * feat), TOKEN_AXES, 0, 0, tiled=True
    ).reshape(rows, 2 * feat)
    x_rows = recv[:, :feat]
    s_rows = recv[:, feat:]
    partial = jnp.concatenate(
        [
            dot(x_rows, w_gate, ((1,), (0,))).astype(jnp.bfloat16),
            dot(x_rows, w_up, ((1,), (0,))).astype(jnp.bfloat16),
            dot(s_rows, w_down, ((1,), (1,))).astype(jnp.bfloat16),
        ],
        axis=1,
    )
    total = scatter_sum(partial)
    gate = total[:, :ff]
    up = total[:, ff : 2 * ff]
    hidden_grad = total[:, 2 * ff :]
    sig = jax.nn.sigmoid(gate)
    act = gate * sig
    part = jnp.concatenate(
        [act * up, hidden_grad * up * sig * (1.0 + gate * (1.0 - sig)), hidden_grad * act], axis=1
    ).astype(jnp.bfloat16)
    full = gather_rows(part)
    hidden = full[:, :ff]
    gate_grad = full[:, ff : 2 * ff]
    up_grad = full[:, 2 * ff :]
    expert_out = dot(hidden, w_down, ((1,), (0,)))
    row_grad = dot(gate_grad, w_gate, ((1,), (1,))) + dot(up_grad, w_up, ((1,), (1,)))
    back = jnp.concatenate([expert_out, row_grad], axis=1).astype(jnp.bfloat16)
    back = lax.all_to_all(
        back.reshape(experts, room, 2 * feat), TOKEN_AXES, 0, 0, tiled=True
    ).reshape(rows, 2 * feat)
    grad_gate = dot(x_rows, gate_grad, ((0,), (0,)))
    grad_up = dot(x_rows, up_grad, ((0,), (0,)))
    grad_down = dot(hidden, s_rows, ((0,), (0,)))
    out = dot(dispatch, back, ((0,), (0,)))
    layer_out = (router_weight[:, None] * out[:, :feat]).astype(jnp.bfloat16)
    grad_tokens = out[:, feat:].astype(jnp.bfloat16)
    return (
        layer_out,
        grad_tokens,
        jnp.stack([grad_gate, grad_up]).astype(jnp.bfloat16)[None],
        grad_down.astype(jnp.bfloat16)[None],
    )


def solution(mesh):
    fine = Mesh(mesh.devices.reshape(NZ, NX, 2, 8, 2), ("zh", "x", "zl", "y", "core"))
    dp = ("zh", "x")
    ex = TOKEN_AXES
    return jax.shard_map(
        shards,
        mesh=fine,
        in_specs=(P(ex, dp), P(ex), P(ex), P(ex, dp), P(ex, None, dp, None), P(ex, None, dp)),
        out_specs=(P(ex, dp), P(ex, dp), P(ex, None, dp, None), P(ex, None, dp)),
        check_vma=False,
    )
```

profile of v0, /device:TPU:8, one launch (start us, length us, event | category | flops | bytes accessed | tf_op | source)
XLA Modules:
  0.0 203.6 jit_solution(1716345662355274634)
XLA Ops:
  7.2 0.9 convert_reduce_fusion
  8.2 0.7 multiply_add_fusion
  8.9 1.3 convolution_convert_fusion.7
  10.2 1.2 convolution_convert_fusion.8
  11.5 0.1 pad_maximum_fusion.2
  11.5 32.7 %all_to_all.20 = bf16[32,12,768]{2,1,0:T(8,128)(2,1)S(1)} all-to-all(bf16[32,12,768]{2,1,0:T(8,128)(2,1)S(1)} %pad_maximum_fusion.2), channel_id=1, replica_groups=mesh['zh'=4,'x'=4,'zl'=2,'y'=8,'core'=2] {'zl','y','core'}, dimensions={0} | all-to-all | bytes 1179648 | tf_op jit(solution)/shard_map/all_to_all | solution.py:55
  44.2 0.1 reshape.84
  44.4 1.8 convolution_convert_fusion.4
  46.2 0.6 convolution_convert_fusion.5
  46.8 0.6 convolution_convert_fusion.3
  47.4 0.2 pad_maximum_fusion
  47.6 32.9 %all_to_all.21 = bf16[4,96,3072]{2,1,0:T(8,128)(2,1)S(1)} all-to-all(bf16[4,96,3072]{2,1,0:T(8,128)(2,1)S(1)} %bitcast.28), channel_id=1, replica_groups=mesh['zh'=4,'x'=4,'zl'=2,'y'=8,'core'=2] {'x'}, dimensions={0} | all-to-all | bytes 4718592 | tf_op jit(solution)/shard_map/all_to_all | solution.py:31
  80.5 0.3 add_convert_fusion
  80.8 25.2 %all_to_all.22 = bf16[4,24,3072]{2,1,0:T(8,128)(2,1)S(1)} all-to-all(bf16[4,24,3072]{2,1,0:T(8,128)(2,1)S(1)} %bitcast.29), channel_id=1, replica_groups=mesh['zh'=4,'x'=4,'zl'=2,'y'=8,'core'=2] {'zh'}, dimensions={0} | all-to-all | bytes 1179648 | tf_op jit(solution)/shard_map/all_to_all | solution.py:33
  106.2 15.8 %all_gather.6 = bf16[96,3072]{1,0:T(8,128)(2,1)} all-gather(bf16[24,3072]{1,0:T(8,128)(2,1)S(1)} %pad_maximum_fusion.4), channel_id=1, replica_groups=mesh['zh'=4,'x'=4,'zl'=2,'y'=8,'core'=2] {'zh'}, dimensions={0}, use_global_device_ids=true | all-gather | bytes 737280 | tf_op jit(solution)/shard_map/all_gather | solution.py:38
  121.9 34.1 %all-gather.2.cloned.1.call-done = bf16[384,3072]{1,0:T(8,128)(2,1)} async-done(((bf16[96,3072]{1,0:T(8,128)(2,1)}), bf16[384,3072]{1,0:T(8,128)(2,1)}) %all-gather.2.cloned.1.call-update) | async-done | bytes 2359312 | tf_op jit(solution)/shard_map/all_gather | solution.py:38
  156.0 1.7 fusion.8
  157.8 1.7 fusion.3
  159.7 1.2 slice.94
  160.8 0.2 dot_general.43
  161.0 0.6 convolution_convert_fusion.6
  161.7 1.2 copy.18
  162.9 8.5 %all-to-all-start.3 = ((bf16[32,12,768]{2,1,0:T(8,128)(2,1)}), bf16[32,12,768]{2,1,0:T(8,128)(2,1)S(1)}, u32[]{:S(2)}, u32[]{:S(2)}) async-start(bf16[32,12,768]{2,1,0:T(8,128)(2,1)} %copy.18), calls=%async_computation.3 | async-start | bytes 1572864 | tf_op jit(solution)/shard_map/all_to_all | solution.py:84
  171.5 1.7 fusion
  173.2 1.7 fusion.1
  174.9 1.3 pad_maximum_fusion.1
  176.2 2.7 %fusion.2 = bf16[1,1024,384]{2,1,0:T(8,128)(2,1)} fusion(bf16[384,768]{1,0:T(8,128)(2,1)S(1)} %reshape.84, bf16[384,3072]{1,0:T(8,128)(2,1)} %all-gather.2.cloned.1.call-done), kind=kOutput, calls=%fused_computation.10 | convolution fusion | flops 302383104 | bytes 1867776 | tf_op jit(solution)/shard_map/dot_general | solution.py:21
  178.9 15.9 %all-to-all-done.3 = bf16[32,12,768]{2,1,0:T(8,128)(2,1)S(1)} async-done(((bf16[32,12,768]{2,1,0:T(8,128)(2,1)}), bf16[32,12,768]{2,1,0:T(8,128)(2,1)S(1)}, u32[]{:S(2)}, u32[]{:S(2)}) %all-to-all-start.3) | async-done | bytes 589856 | tf_op jit(solution)/shard_map/all_to_all | solution.py:84
  194.8 0.1 reshape.86
  195.0 0.4 fusion.20
  195.4 0.7 slice.159
  196.0 0.8 fusion.21
  (16 shorter events, 0.5 us)
Async XLA Ops:
  7.2 39.6 %copy-start = (bf16[1,1024,384]{2,1,0:T(8,128)(2,1)S(1)}, bf16[1,1024,384]{2,1,0:T(8,128)(2,1)}, u32[]{:S(2)}) copy-start(bf16[1,1024,384]{2,1,0:T(8,128)(2,1)} %param.11) | copy-start | bytes 2359300
  7.2 148.8 %all-gather.2.cloned.1.call-start = ((), (), s32[]{:S(2)}) async-start(), calls=%async_computation.4 | async-start | bytes 2949120 | tf_op jit(solution)/shard_map/all_gather | solution.py:38
  44.4 1.8 copy-start.2
  162.9 31.9 %all-to-all-start.3 = ((bf16[32,12,768]{2,1,0:T(8,128)(2,1)}), bf16[32,12,768]{2,1,0:T(8,128)(2,1)S(1)}, u32[]{:S(2)}, u32[]{:S(2)}) async-start(bf16[32,12,768]{2,1,0:T(8,128)(2,1)} %copy.18), calls=%async_computation.3 | async-start | bytes 1572864 | tf_op jit(solution)/shard_map/all_to_all | solution.py:84
  178.9 17.1 %copy-start.1 = (f32[192]{0:T(256)S(1)}, f32[192]{0:T(256)}, u32[]{:S(2)}) copy-start(f32[192]{0:T(256)} %param.8) | copy-start | bytes 2308
Sparse Core Ops, SparseCore 0:
  122.1 33.9 all-gather.1
where the time goes:
time: 204 us
  blocking collectives  107 us (52%)
  waiting for transfers between devices  50 us (25%)
  matrix products  16.1 us (8%)
  between operations  14.2 us (7%)
  starting transfers between devices  8.55 us (4%)
  other arithmetic  4.44 us (2%)
  local copies, waits for them, and re-layouts  3.8 us (2%)
    all_gather x1, waiting for transfers between devices, gather_rows(): lax.all_gather(lax.all_gather(part, 'zh', axis=0, tiled=True), 'x', axis=...  34.1 us
    all_to_all x1, blocking collectives, scatter_sum(): lax.all_to_all(partial.reshape(NX, rows // NX, width), 'x', 0, 0, tiled=T...  32.9 us
    all_to_all x1, blocking collectives, shards(): lax.all_to_all(send.reshape(experts, room, 2 * feat), TOKEN_AXES, 0, 0, t...  32.7 us
    all_to_all x1, blocking collectives, scatter_sum(): lax.all_to_all(first.reshape(NZ, rows // NX // NZ, width), 'zh', 0, 0, ti...  25.2 us
    dot_general x12, matrix products, dot(): lax.dot_general(a, b, (dims, ((), ())), preferred_element_type=jnp.float32)  16.1 us
    all_to_all x1, waiting for transfers between devices, shards(): lax.all_to_all(back.reshape(experts, room, 2 * feat), TOKEN_AXES, 0, 0, t...  15.9 us
    all_gather x1, blocking collectives, gather_rows(): lax.all_gather(part, 'zh', axis=0, tiled=True)  15.8 us
    all_to_all x1, starting transfers between devices, shards(): lax.all_to_all(back.reshape(experts, room, 2 * feat), TOKEN_AXES, 0, 0, t...  8.51 us
  transfers between devices with their start and end apart: 2, of which 2 were waited for; matrix products, arithmetic and copies ran while one was open for 4% of the time, Pallas kernels for 0%

commit v1 on v0

--- a/solution.py
+++ b/solution.py
@@ -35,7 +35,15 @@
 
 
 def gather_rows(part):
-    return lax.all_gather(lax.all_gather(part, "zh", axis=0, tiled=True), "x", axis=0, tiled=True)
+    return jnp.concatenate(
+        lax.all_to_all(
+            jnp.stack([lax.all_gather(part, "zh", axis=0, tiled=True)] * lax.axis_size("x")),
+            "x",
+            0,
+            0,
+        ),
+        axis=0,
+    )
 
 
 def shards(tokens, expert_of, router_weight, cotangent, gate_up_weight, down_weight):

time: 204 us -> 187 us (0.917)
  waiting for transfers between devices: 50 us -> 18.3 us
  blocking collectives: 107 us -> 136 us
  between operations: 14.2 us -> 0.88 us
  local copies, waits for them, and re-layouts: 3.8 us -> 8.55 us
  starting transfers between devices: 8.55 us -> 4.6 us
  matrix products: 16.1 us -> 13.5 us
    all_gather x1 -> x0, waiting for transfers between devices: 34.1 us -> none  [gather_rows(): lax.all_gather(lax.all_gather(part, 'zh', axis=0, tiled=True), 'x', axis=...]
    all_to_all x0 -> x1, blocking collectives: none -> 30.2 us  [gather_rows(): lax.all_to_all(jnp.stack([lax.all_gather(part, 'zh', axis=0, tiled=True)]...]
    all_to_all x1, starting transfers between devices: 8.51 us -> 4.6 us  [shards(): lax.all_to_all(back.reshape(experts, room, 2 * feat), TOKEN_AXES, 0, 0, t...]
    dot_general x12, matrix products: 16.1 us -> 13.5 us  [dot(): lax.dot_general(a, b, (dims, ((), ())), preferred_element_type=jnp.float32)]
    all_to_all x1, waiting for transfers between devices: 15.9 us -> 18.3 us  [shards(): lax.all_to_all(back.reshape(experts, room, 2 * feat), TOKEN_AXES, 0, 0, t...]
  transfers between devices with their start and end apart: 2 -> 1, of which waited for: 2 -> 1; matrix products, arithmetic and copies ran while one was open for 4% -> 3% of each run, Pallas kernels for 0% -> 0%
where the time goes in v1:
time: 187 us; the launch traced here: 186 us
  blocking collectives  136 us (73%)
  waiting for transfers between devices  18.3 us (10%)
  matrix products  13.5 us (7%)
  local copies, waits for them, and re-layouts  8.55 us (5%)
  starting transfers between devices  4.6 us (2%)
  other arithmetic  4.45 us (2%)
    all_to_all x1, blocking collectives, scatter_sum(): lax.all_to_all(partial.reshape(NX, rows // NX, width), 'x', 0, 0, tiled=T...  32.9 us
    all_to_all x1, blocking collectives, shards(): lax.all_to_all(send.reshape(experts, room, 2 * feat), TOKEN_AXES, 0, 0, t...  32.7 us
    all_to_all x1, blocking collectives, gather_rows(): lax.all_to_all(jnp.stack([lax.all_gather(part, 'zh', axis=0, tiled=True)]...  30.2 us
    all_to_all x1, blocking collectives, scatter_sum(): lax.all_to_all(first.reshape(NZ, rows // NX // NZ, width), 'zh', 0, 0, ti...  25.2 us
    all_to_all x1, waiting for transfers between devices, shards(): lax.all_to_all(back.reshape(experts, room, 2 * feat), TOKEN_AXES, 0, 0, t...  18.3 us
    all_gather x1, blocking collectives, gather_rows(): lax.all_gather(part, 'zh', axis=0, tiled=True)  15 us
    dot_general x12, matrix products, dot(): lax.dot_general(a, b, (dims, ((), ())), preferred_element_type=jnp.float32)  13.5 us
    all_to_all x1, starting transfers between devices, shards(): lax.all_to_all(back.reshape(experts, room, 2 * feat), TOKEN_AXES, 0, 0, t...  4.6 us
  transfers between devices with their start and end apart: 1, of which 1 were waited for; matrix products, arithmetic and copies ran while one was open for 3% of the time, Pallas kernels for 0%

profile of v1, /device:TPU:8, one launch (start us, length us, event | category | flops | bytes accessed | tf_op | source)
XLA Modules:
  0.0 186.3 jit_solution(5914491448121782317)
XLA Ops:
  0.6 0.9 convert_reduce_fusion
  1.6 0.7 multiply_add_fusion
  2.3 1.3 convolution_convert_fusion.7
  3.6 1.2 convolution_convert_fusion.8
  5.0 32.7 %all_to_all.25 = bf16[32,12,768]{2,1,0:T(8,128)(2,1)S(1)} all-to-all(bf16[32,12,768]{2,1,0:T(8,128)(2,1)S(1)} %pad_maximum_fusion.2), channel_id=1, replica_groups=mesh['zh'=4,'x'=4,'zl'=2,'y'=8,'core'=2] {'zl','y','core'}, dimensions={0} | all-to-all | bytes 1179648 | tf_op jit(solution)/shard_map/all_to_all | solution.py:63
  37.8 1.9 %convolution_convert_fusion.4 = bf16[384,1024]{1,0:T(8,128)(2,1)S(1)} fusion(bf16[1,2,384,1024]{3,2,1,0:T(8,128)(2,1)} %param.10, bf16[384,768]{1,0:T(8,128)(2,1)S(1)} %reshape.89), kind=kOutput, calls=%fused_computation.6 | convolution fusion | flops 302383104 | bytes 1867776 | tf_op jit(solution)/shard_map/dot_general | solution.py:21
  39.8 0.6 convolution_convert_fusion.5
  40.4 0.6 convolution_convert_fusion.3
  41.1 32.9 %all_to_all.26 = bf16[4,96,3072]{2,1,0:T(8,128)(2,1)S(1)} all-to-all(bf16[4,96,3072]{2,1,0:T(8,128)(2,1)S(1)} %bitcast.29), channel_id=1, replica_groups=mesh['zh'=4,'x'=4,'zl'=2,'y'=8,'core'=2] {'x'}, dimensions={0} | all-to-all | bytes 4718592 | tf_op jit(solution)/shard_map/all_to_all | solution.py:31
  74.0 0.3 add_convert_fusion
  74.4 25.2 %all_to_all.27 = bf16[4,24,3072]{2,1,0:T(8,128)(2,1)S(1)} all-to-all(bf16[4,24,3072]{2,1,0:T(8,128)(2,1)S(1)} %bitcast.36), channel_id=1, replica_groups=mesh['zh'=4,'x'=4,'zl'=2,'y'=8,'core'=2] {'zh'}, dimensions={0} | all-to-all | bytes 1179648 | tf_op jit(solution)/shard_map/all_to_all | solution.py:33
  99.7 15.0 %all_gather.3 = bf16[96,3072]{1,0:T(8,128)(2,1)S(1)} all-gather(bf16[24,3072]{1,0:T(8,128)(2,1)S(1)} %pad_maximum_fusion.4), channel_id=1, replica_groups=mesh['zh'=4,'x'=4,'zl'=2,'y'=8,'core'=2] {'zh'}, dimensions={0}, use_global_device_ids=true | all-gather | bytes 737280 | tf_op jit(solution)/shard_map/all_gather | solution.py:40
  114.7 0.3 stack.16
  115.0 30.2 %all_to_all.28 = bf16[4,96,3072]{2,1,0:T(8,128)(2,1)S(1)} all-to-all(bf16[4,96,3072]{2,1,0:T(8,128)(2,1)S(1)} %stack.16), channel_id=1, replica_groups=mesh['zh'=4,'x'=4,'zl'=2,'y'=8,'core'=2] {'x'}, dimensions={0} | all-to-all | bytes 4718592 | tf_op jit(solution)/shard_map/all_to_all | solution.py:39
  145.2 0.6 fusion.8
  145.8 0.9 slice.94
  146.7 1.3 fusion.3
  148.0 1.0 concatenate.36
  149.1 0.8 copy.17
  149.8 2.1 %dot_general.43 = bf16[32,12,1024]{2,1,0:T(8,128)(2,1)} reshape(bf16[384,1024]{1,0:T(8,128)(2,1)} %slice.94) | data formatting | bytes 1572864 | tf_op jit(solution)/shard_map/dot_general | solution.py:21
  151.9 1.9 %convolution_convert_fusion.6 = bf16[32,12,384]{2,0,1:T(8,128)(2,1)S(1)} fusion(bf16[1,1024,384]{2,1,0:T(8,128)(2,1)S(1)} %copy-done, bf16[32,12,1024]{2,1,0:T(8,128)(2,1)} %dot_general.43), kind=kOutput, calls=%fused_computation.13 | convolution fusion | flops 302137344 | bytes 1867776 | tf_op jit(solution)/shard_map/dot_general | solution.py:21
  153.9 1.2 copy.18
  155.1 4.6 %all-to-all-start.4 = ((bf16[32,12,768]{2,1,0:T(8,128)(2,1)}), bf16[32,12,768]{2,1,0:T(8,128)(2,1)}, u32[]{:S(2)}, u32[]{:S(2)}) async-start(bf16[32,12,768]{2,1,0:T(8,128)(2,1)} %copy.18), calls=%async_computation.4 | async-start | bytes 1572864 | tf_op jit(solution)/shard_map/all_to_all | solution.py:92
  159.7 1.6 fusion
  161.4 0.6 fusion.1
  162.0 1.3 pad_maximum_fusion.1
  163.3 1.6 fusion.2
  164.8 18.3 %all-to-all-done.4 = bf16[32,12,768]{2,1,0:T(8,128)(2,1)} async-done(((bf16[32,12,768]{2,1,0:T(8,128)(2,1)}), bf16[32,12,768]{2,1,0:T(8,128)(2,1)}, u32[]{:S(2)}, u32[]{:S(2)}) %all-to-all-start.4) | async-done | bytes 589856 | tf_op jit(solution)/shard_map/all_to_all | solution.py:92
  183.2 1.3 reshape.92
  184.4 0.4 fusion.20
  184.8 0.7 slice.159
  185.5 0.8 fusion.21
  (21 shorter events, 0.7 us)
Async XLA Ops:
  0.6 39.7 %copy-start = (bf16[1,1024,384]{2,1,0:T(8,128)(2,1)S(1)}, bf16[1,1024,384]{2,1,0:T(8,128)(2,1)}, u32[]{:S(2)}) copy-start(bf16[1,1024,384]{2,1,0:T(8,128)(2,1)} %param.11) | copy-start | bytes 2359300
  37.8 2.6 %copy-start.1 = (bf16[384,768]{1,0:T(8,128)(2,1)}, bf16[384,768]{1,0:T(8,128)(2,1)S(1)}, u32[]{:S(2)}) copy-start(bf16[384,768]{1,0:T(8,128)(2,1)S(1)} %reshape.89) | copy-start | bytes 1769476
  37.8 2.0 %copy-start.5 = (bf16[1,2,384,1024]{3,2,1,0:T(8,128)(2,1)S(1)}, bf16[1,2,384,1024]{3,2,1,0:T(8,128)(2,1)}, u32[]{:S(2)}) copy-start(bf16[1,2,384,1024]{3,2,1,0:T(8,128)(2,1)} %param.10) | copy-start | bytes 4718596
  151.9 1.9 %copy-start.3 = (bf16[32,12,384]{2,0,1:T(8,128)(2,1)S(1)}, bf16[32,12,384]{2,0,1:T(8,128)(2,1)}, u32[]{:S(2)}) copy-start(bf16[32,12,384]{2,0,1:T(8,128)(2,1)} %copy.17) | copy-start | bytes 884740
  155.1 28.0 %all-to-all-start.4 = ((bf16[32,12,768]{2,1,0:T(8,128)(2,1)}), bf16[32,12,768]{2,1,0:T(8,128)(2,1)}, u32[]{:S(2)}, u32[]{:S(2)}) async-start(bf16[32,12,768]{2,1,0:T(8,128)(2,1)} %copy.18), calls=%async_computation.4 | async-start | bytes 1572864 | tf_op jit(solution)/shard_map/all_to_all | solution.py:92
  159.7 1.6 copy-start.2
  164.8 20.7 %copy-start.4 = (f32[192]{0:T(256)S(1)}, f32[192]{0:T(256)}, u32[]{:S(2)}) copy-start(f32[192]{0:T(256)} %param.8) | copy-start | bytes 2308
